TPU v7x, 256 devices: a whole 4x4x8 slice. The times are simulated.
256 devices in a mesh: depth: 32 (over x, y, z_lo), kslab: 8 (over z_hi, core).
Axes of the slice: x: 4, y: 4, z: 8 (z_hi: 4, z_lo: 2; z = z_hi * 2 + z_lo), core: 2. Of those that a mesh axis runs over, the one named last changes fastest.
Arguments:
- spectra: bfloat16 [32, 2, 512, 1024], P('depth', None, 'kslab'), may hold values from -6 to 6
- green: bfloat16 [32, 32, 2, 512, 1024], P('depth', None, None, 'kslab'), may hold values from -1 to 1, as said below
- contrast: float32 [32, 512, 1024], P('depth', None, 'kslab'), may hold values from 0.3 to 3
Outputs:
- applied: bfloat16 [32, 2, 512, 1024], P('depth', None, None, 'kslab')
Inputs may be any that keep to these rules, and one draw needn't show every extreme that they name: green[t, s] equals green[s, t] for every pair of layers (reciprocity).
All inputs are finite; a program needn't handle non-finite values.
Results may differ from a plain program's by a relative error of at most 0.007.
Values may be sent and summed in bfloat16 or wider, within the bound.
A program may use at most 128 MiB of HBM per device.

v0:
```python
import math

import jax
import jax.numpy as jnp
from jax import lax
from jax.sharding import PartitionSpec as P

NX = 512
NY = 1024


def fourier_tables(length):
    indices = jnp.arange(length, dtype=jnp.int32)
    products = indices[:, None] * indices[None, :] % length
    angles = products.astype(jnp.float32) * (2.0 * math.pi / length)
    factor = 1.0 / math.sqrt(length)
    return (
        (jnp.cos(angles) * factor).astype(jnp.bfloat16),
        (jnp.sin(angles) * factor).astype(jnp.bfloat16),
    )


def on_device(spectra, green, contrast):
    lay_dev = spectra.shape[0]
    kx_dev = spectra.shape[2]
    coeffs = green.astype(jnp.float32)
    sources = lax.all_gather(spectra, "depth", axis=0, tiled=True).astype(jnp.float32)[None]
    real_part = jnp.sum(
        coeffs[:, :, 0] * sources[:, :, 0] - coeffs[:, :, 1] * sources[:, :, 1], axis=1
    )
    imag_part = jnp.sum(
        coeffs[:, :, 0] * sources[:, :, 1] + coeffs[:, :, 1] * sources[:, :, 0], axis=1
    )
    summed = jnp.stack([real_part, imag_part], axis=1)
    rounded = summed.astype(jnp.bfloat16)
    cos_y, sin_y = fourier_tables(NY)
    table_y = jnp.concatenate([cos_y, sin_y], axis=1)
    row_total = lay_dev * kx_dev
    from_real = jnp.dot(
        rounded[:, 0].reshape(row_total, NY), table_y, preferred_element_type=jnp.float32
    )
    from_imag = jnp.dot(
        rounded[:, 1].reshape(row_total, NY), table_y, preferred_element_type=jnp.float32
    )
    halfway_real = (from_real[:, :NY] - from_imag[:, NY:]).reshape(lay_dev, kx_dev, NY)
    halfway_imag = (from_real[:, NY:] + from_imag[:, :NY]).reshape(lay_dev, kx_dev, NY)
    halfway = jnp.stack([halfway_real, halfway_imag], axis=1).astype(jnp.bfloat16)
    cos_x, sin_x = fourier_tables(NX)
    table_x = jnp.concatenate([cos_x, sin_x], axis=0)
    stacked = jnp.einsum(
        "ak,nckd->ncad",
        table_x,
        lax.all_to_all(halfway, "kslab", split_axis=3, concat_axis=2, tiled=True),
        preferred_element_type=jnp.float32,
    )
    real_part = stacked[:, 0, :NX] - stacked[:, 1, NX:]
    imag_part = stacked[:, 0, NX:] + stacked[:, 1, :NX]
    field_out = jnp.stack([real_part, imag_part], axis=1)
    return (field_out * contrast[:, None]).astype(jnp.bfloat16)


def solution(mesh):
    in_specs = (
        P("depth", None, "kslab", None),
        P("depth", None, None, "kslab", None),
        P("depth", None, "kslab"),
    )
    out_specs = P("depth", None, None, "kslab")
    return jax.shard_map(
        on_device, mesh=mesh, in_specs=in_specs, out_specs=out_specs, check_vma=False
    )
```

profile of v0, /device:TPU:1, one launch (start us, length us, event | category | flops | bytes accessed | tf_op | source)
XLA Modules:
  0.0 259.9 jit_solution(13273362459274215923)
XLA Ops:
  6.5 0.0 all-gather.2.cloned.1.call-start
  6.5 0.7 all-gather.2.cloned.1.call-update
  7.3 11.3 %convert_element_type.55 = f32[1,32,2,64,1024]{4,3,2,1,0:T(8,128)} convert(bf16[1,32,2,64,1024]{4,3,2,1,0:T(8,128)(2,1)} %param.4) | non-fusion elementwise | flops 4194304 | bytes 25165824 | tf_op jit(solution)/shard_map/convert_element_type | solution.py:26
  18.6 17.9 %multiply_convert_fusion = (bf16[1024,1024]{1,0:T(8,128)(2,1)S(1)}, bf16[1024,1024]{1,0:T(8,128)(2,1)}) fusion(), kind=kLoop, calls=%fused_computation.10 | loop fusion | flops 18874368 | bytes 4194304 | tf_op jit(solution)/shard_map/convert_element_type | solution.py:19
  36.5 169.1 %all-gather.2.cloned.1.call-done = bf16[32,2,64,1024]{3,2,1,0:T(8,128)(2,1)} async-done(((bf16[1,2,64,1024]{3,2,1,0:T(8,128)(2,1)}), bf16[32,2,64,1024]{3,2,1,0:T(8,128)(2,1)}) %all-gather.2.cloned.1.call-update) | async-done | bytes 8388624 | tf_op jit(solution)/shard_map/all_gather | solution.py:27
  205.5 11.3 %bitcast_convert_fusion = f32[1,32,2,64,1024]{4,3,2,1,0:T(8,128)} fusion(bf16[32,2,64,1024]{3,2,1,0:T(8,128)(2,1)} %all-gather.2.cloned.1.call-done), kind=kLoop, calls=%fused_computation | loop fusion | flops 4194304 | bytes 25165824 | tf_op jit(solution)/shard_map/broadcast_in_dim | solution.py:27
  216.9 0.0 copy-start
  216.9 13.0 %subtract_reduce_fusion = (bf16[64,1024]{1,0:T(8,128)(2,1)S(1)}, bf16[64,1024]{1,0:T(8,128)(2,1)S(1)}) fusion(f32[1,32,2,64,1024]{4,3,2,1,0:T(8,128)} %bitcast_convert_fusion, f32[1,32,2,64,1024]{4,3,2,1,0:T(8,128)} %convert_element_type.55), kind=kLoop, calls=%fused_computation.2 | loop fusion | flops 16646144 | bytes 33816576 | tf_op jit(solution)/shard_map/reduce_sum | solution.py:28
  229.8 0.0 copy-done
  229.8 0.8 fusion.7
  230.7 0.0 copy-start.1
  230.7 0.8 fusion.6
  231.6 0.1 fusion.19
  231.7 0.4 copy.15
  232.1 1.1 reshape.229
  233.2 6.9 %all-to-all-start = ((bf16[8,2,8192]{2,1,0:T(2,128)(2,1)}), bf16[8,2,8192]{2,1,0:T(2,128)(2,1)S(1)}, u32[]{:S(2)}, u32[]{:S(2)}) async-start(bf16[8,2,8192]{2,1,0:T(2,128)(2,1)} %reshape.229), calls=%async_computation | async-start | bytes 524288 | tf_op jit(solution)/shard_map/all_to_all | solution.py:53
  240.1 0.0 copy-done.1
  240.1 0.1 copy.19
  240.2 4.4 %multiply_convert_fusion.2 = (bf16[512,512]{1,0:T(8,128)(2,1)S(1)}, bf16[512,512]{1,0:T(8,128)(2,1)S(1)}) fusion(), kind=kLoop, calls=%fused_computation.27 | loop fusion | flops 4718592 | bytes 1048576 | tf_op jit(solution)/shard_map/convert_element_type | solution.py:19
  244.6 6.2 %all-to-all-done = bf16[8,2,8192]{2,1,0:T(2,128)(2,1)S(1)} async-done(((bf16[8,2,8192]{2,1,0:T(2,128)(2,1)}), bf16[8,2,8192]{2,1,0:T(2,128)(2,1)S(1)}, u32[]{:S(2)}, u32[]{:S(2)}) %all-to-all-start) | async-done | bytes 262176 | tf_op jit(solution)/shard_map/all_to_all | solution.py:53
  250.8 0.3 reshape.230
  251.2 0.4 copy.23
  251.6 0.5 convolution_bitcast_fusion
  252.1 0.1 slice_subtract_fusion
  252.2 0.1 fusion.16
  252.3 0.8 copy.20
  (1 shorter events, 0.0 us)
Async XLA Ops:
  6.5 199.0 %all-gather.2.cloned.1.call-start = ((), (), s32[]{:S(2)}) async-start(), calls=%async_computation.1 | async-start | bytes 8650752 | tf_op jit(solution)/shard_map/all_gather | solution.py:27
  216.9 13.0 %copy-start = (bf16[1024,1024]{1,0:T(8,128)(2,1)S(1)}, bf16[1024,1024]{1,0:T(8,128)(2,1)}, u32[]{:S(2)}) copy-start(bf16[1024,1024]{1,0:T(8,128)(2,1)} %get-tuple-element.12) | copy-start | bytes 6291460
  230.7 9.4 %copy-start.1 = (f32[1,512,128]{2,1,0:T(8,128)S(1)}, f32[1,512,128]{2,1,0:T(8,128)}, u32[]{:S(2)}) copy-start(f32[1,512,128]{2,1,0:T(8,128)} %param.5) | copy-start | bytes 786436
  233.2 17.7 %all-to-all-start = ((bf16[8,2,8192]{2,1,0:T(2,128)(2,1)}), bf16[8,2,8192]{2,1,0:T(2,128)(2,1)S(1)}, u32[]{:S(2)}, u32[]{:S(2)}) async-start(bf16[8,2,8192]{2,1,0:T(2,128)(2,1)} %reshape.229), calls=%async_computation | async-start | bytes 524288 | tf_op jit(solution)/shard_map/all_to_all | solution.py:53
Sparse Core Ops, SparseCore 0:
  9.1 196.3 all-gather.1
where the time goes:
time: 260 us
  waiting for transfers between devices  176 us (68%)
  other arithmetic  58.1 us (22%)
  between operations  13.5 us (5%)
  starting transfers between devices  6.93 us (3%)
  local copies, waits for them, and re-layouts  3.21 us (1%)
    all_gather x1, waiting for transfers between devices, on_device(): lax.all_gather(spectra, 'depth', axis=0, tiled=True).astype(jnp.float32)  169 us
    convert_element_type x2, other arithmetic, fourier_tables(): (jnp.sin(angles) * factor).astype(jnp.bfloat16)  22.3 us
    reduce_sum x1, other arithmetic, on_device(): jnp.sum(coeffs[:, :, 0] * sources[:, :, 0] - coeffs[:, :, 1] * sources[:,...  13 us
    convert_element_type x1, other arithmetic, on_device(): coeffs = green.astype(jnp.float32)  11.3 us
    broadcast_in_dim x1, other arithmetic, on_device(): lax.all_gather(spectra, 'depth', axis=0, tiled=True).astype(jnp.float32)  11.3 us
    all_to_all x1, starting transfers between devices, on_device(): lax.all_to_all(halfway, 'kslab', split_axis=3, concat_axis=2, tiled=True)  6.93 us
    all_to_all x1, waiting for transfers between devices, on_device(): lax.all_to_all(halfway, 'kslab', split_axis=3, concat_axis=2, tiled=True)  6.22 us
  transfers between devices with their start and end apart: 2, of which 2 were waited for; matrix products, arithmetic and copies ran while one was open for 13% of the time, Pallas kernels for 0%

commit v1 on v0

v1 whole, which is shorter than its diff:
```python
import functools
import math

import jax
import jax.numpy as jnp
import ml_dtypes
import numpy as np
from jax import lax
from jax.experimental import pallas as pl
from jax.experimental.pallas import tpu as pltpu
from jax.sharding import PartitionSpec as P

NX = 512
NY = 1024
LAYERS = 32
SLABS = 8
ROWS = NX // SLABS
COLS = NY // SLABS
CHUNKS = 2
R = ROWS // CHUNKS
MESH = pl.DeviceIdType.MESH


def fourier_tables(length):
    indices = np.arange(length, dtype=np.int64)
    products = indices[:, None] * indices[None, :] % length
    angles = products.astype(np.float64) * (2.0 * math.pi / length)
    factor = 1.0 / math.sqrt(length)
    return (
        (np.cos(angles) * factor).astype(np.float32).astype(ml_dtypes.bfloat16),
        (np.sin(angles) * factor).astype(np.float32).astype(ml_dtypes.bfloat16),
    )


def kernel(
    spectra, green, contrast, table_y, table_x, out,
    held, coeffs, ty, tx, con, summed, outgoing, halves,
    own_sem, load_sem, send_sem, recv_sem, swap_send, swap_recv,
):
    depth = lax.axis_index("depth")
    slab = lax.axis_index("kslab")
    at_x, at_y, at_z = depth // 8, (depth // 2) % 4, depth % 2

    def own_copy(c, p):
        return pltpu.make_async_copy(
            spectra.at[0, p, pl.ds(c * R, R)], held.at[c, p, depth], own_sem.at[c, p]
        )

    for c in range(CHUNKS):
        for p in range(2):
            own_copy(c, p).start()
    loads = [
        pltpu.make_async_copy(green.at[0], coeffs, load_sem.at[0]),
        pltpu.make_async_copy(table_y, ty, load_sem.at[1]),
        pltpu.make_async_copy(table_x, tx, load_sem.at[2]),
        pltpu.make_async_copy(contrast.at[0], con, load_sem.at[3]),
    ]
    for load in loads:
        load.start()

    def layer(p, dz, da, db):
        ca = at_x * (1 - p) + at_y * p
        cb = at_y * (1 - p) + at_x * p
        return (
            (ca + da + 4) % 4 * (8 - 6 * p)
            + (cb + db + 4) % 4 * (2 + 6 * p)
            + (at_z + dz) % 2
        )

    barrier = pltpu.get_barrier_semaphore()
    for other in (
        layer(0, 1, 0, 0), layer(0, 0, 1, 0), layer(0, 0, -1, 0),
        layer(0, 0, 0, 1), layer(0, 0, 0, -1),
    ):
        pl.semaphore_signal(
            barrier, inc=1, device_id={"depth": other}, device_id_type=MESH
        )
    for k in range(1, SLABS):
        pl.semaphore_signal(
            barrier, inc=1, device_id={"kslab": (slab + k) % SLABS}, device_id_type=MESH
        )
    pl.semaphore_wait(barrier, 5 + SLABS - 1)

    def send(c, p, block, to, half=None):
        ref = held.at[c, p, block]
        if half is not None:
            ref = held.at[c, p, block, pl.ds(half * (R // 2), R // 2)]
        pltpu.make_async_remote_copy(
            src_ref=ref, dst_ref=ref,
            send_sem=send_sem.at[c, p], recv_sem=recv_sem.at[c, p, block],
            device_id={"depth": to}, device_id_type=MESH,
        ).start()

    def arrived(c, p, block):
        ref = held.at[c, p, block]
        pltpu.make_async_remote_copy(
            src_ref=ref, dst_ref=ref,
            send_sem=send_sem.at[c, p], recv_sem=recv_sem.at[c, p, block],
            device_id={"depth": layer(0, 1, 0, 0)}, device_id_type=MESH,
        ).wait_recv()

    def along_a(c, p, block):
        send(c, p, block, layer(p, 0, 1, 0))
        send(c, p, block, layer(p, 0, -1, 0))

    def along_b(c, p, block):
        send(c, p, block, layer(p, 0, 0, 1))
        send(c, p, block, layer(p, 0, 0, -1))

    def both_parts(step):
        def body(p, carry):
            step(p)
            return carry
        lax.fori_loop(0, 2, body, 0)

    def first(c):
        def step(p):
            own_copy(c, p).wait()
            send(c, p, depth, layer(p, 1, 0, 0))
            along_a(c, p, depth)
        both_parts(step)
        both_parts(lambda p: along_b(c, p, depth))

    def partner(c):
        def step(p):
            block = layer(p, 1, 0, 0)
            arrived(c, p, block)
            along_a(c, p, block)
            along_b(c, p, block)
        both_parts(step)

    def near(c, dz):
        def step(p):
            before, after = layer(p, dz, -1, 0), layer(p, dz, 1, 0)
            arrived(c, p, before)
            send(c, p, before, layer(p, 0, 1, 0), 0)
            arrived(c, p, after)
            send(c, p, after, layer(p, 0, -1, 0), 1)
            along_b(c, p, before)
            along_b(c, p, after)
        both_parts(step)

    def far(c, dz):
        def step(p):
            block = layer(p, dz, 2, 0)
            arrived(c, p, block)
            along_b(c, p, block)
        both_parts(step)

    def relay(c, da):
        def step(p):
            def each(dz, carry):
                before, after = layer(p, dz, da, -1), layer(p, dz, da, 1)
                arrived(c, p, before)
                send(c, p, before, layer(p, 0, 0, 1), 0)
                arrived(c, p, after)
                send(c, p, after, layer(p, 0, 0, -1), 1)
                return carry
            lax.fori_loop(0, 2, each, 0)
        both_parts(step)

    def last(c):
        def step(p):
            def each(i, carry):
                arrived(c, p, layer(p, i // 4, i % 4, 2))
                return carry
            lax.fori_loop(0, 8, each, 0)
        both_parts(step)

    def contract(c):
        def column(j, carry):
            cs = pl.ds(pl.multiple_of(j * 128, 128), 128)

            def body(s, acc):
                gr = coeffs[s, 0, pl.ds(c * R, R), cs].astype(jnp.float32)
                gi = coeffs[s, 1, pl.ds(c * R, R), cs].astype(jnp.float32)
                xr = held[c, 0, s, :, cs].astype(jnp.float32)
                xi = held[c, 1, s, :, cs].astype(jnp.float32)
                return acc[0] + (gr * xr - gi * xi), acc[1] + (gr * xi + gi * xr)

            zero = jnp.zeros((R, 128), jnp.float32)
            re, im = lax.fori_loop(0, LAYERS, body, (zero, zero), unroll=4)
            summed[pl.ds(0, R), cs] = re.astype(jnp.bfloat16)
            summed[pl.ds(R, R), cs] = im.astype(jnp.bfloat16)
            return carry
        lax.fori_loop(0, NY // 128, column, 0)

    def swap(c, to):
        return pltpu.make_async_remote_copy(
            src_ref=outgoing.at[c, to], dst_ref=halves.at[slab, c],
            send_sem=swap_send.at[c, to], recv_sem=swap_recv.at[c, slab],
            device_id={"kslab": to}, device_id_type=MESH,
        )

    def transform_y(c):
        def piece(j):
            both = jnp.dot(summed[...], ty[j], preferred_element_type=jnp.float32)
            re = both[:R, :COLS] - both[R:, COLS:]
            im = both[:R, COLS:] + both[R:, :COLS]
            return jnp.concatenate([re, im], axis=1).astype(jnp.bfloat16)

        def each(k, carry):
            to = (slab + k) % SLABS
            outgoing[c, to] = piece(to)
            swap(c, to).start()
            return carry
        lax.fori_loop(1, SLABS, each, 0)
        halves[slab, c] = piece(slab)

    first(0)
    partner(0)
    near(0, 0)
    near(0, 1)
    for c in range(CHUNKS):
        more = c + 1 < CHUNKS
        relay(c, 0)
        far(c, 0)
        far(c, 1)
        if more:
            first(c + 1)
        relay(c, -1)
        relay(c, 1)
        if more:
            partner(c + 1)
        relay(c, 2)
        if more:
            near(c + 1, 0)
        last(c)
        if more:
            near(c + 1, 1)
        if c == 0:
            for load in loads:
                load.wait()
        contract(c)
        transform_y(c)

    for c in range(CHUNKS):
        def each(k, carry, c=c):
            origin = (slab + k) % SLABS
            pltpu.make_async_remote_copy(
                src_ref=outgoing.at[c, origin], dst_ref=halves.at[origin, c],
                send_sem=swap_send.at[c, origin], recv_sem=swap_recv.at[c, origin],
                device_id={"kslab": origin}, device_id_type=MESH,
            ).wait_recv()
            return carry
        lax.fori_loop(1, SLABS, each, 0)

    incoming = halves[...].reshape(NX, 2 * COLS)
    for i in range(4):
        rows = pl.ds(i * 128, 128)
        low = pl.ds(NX + i * 128, 128)
        by_cos = jnp.dot(tx[rows], incoming, preferred_element_type=jnp.float32)
        by_sin = jnp.dot(tx[low], incoming, preferred_element_type=jnp.float32)
        scale = con[rows]
        out[0, 0, rows] = ((by_cos[:, :COLS] - by_sin[:, COLS:]) * scale).astype(jnp.bfloat16)
        out[0, 1, rows] = ((by_sin[:, :COLS] + by_cos[:, COLS:]) * scale).astype(jnp.bfloat16)

    for c in range(CHUNKS):
        for p in range(2):
            sent = held.at[c, p, pl.ds(0, LAYERS - 1)]
            pltpu.make_async_remote_copy(
                src_ref=sent, dst_ref=sent,
                send_sem=send_sem.at[c, p], recv_sem=recv_sem.at[c, p, 0],
                device_id={"depth": layer(0, 1, 0, 0)}, device_id_type=MESH,
            ).wait_send()

        def each(k, carry, c=c):
            swap(c, (slab + k) % SLABS).wait_send()
            return carry
        lax.fori_loop(1, SLABS, each, 0)


def on_device(spectra, green, contrast):
    cos_y, sin_y = fourier_tables(NY)
    table_y = np.stack(
        [
            np.concatenate(
                [cos_y[:, j * COLS:(j + 1) * COLS], sin_y[:, j * COLS:(j + 1) * COLS]], axis=1
            )
            for j in range(SLABS)
        ]
    )
    cos_x, sin_x = fourier_tables(NX)
    table_x = np.concatenate([cos_x, sin_x], axis=0)
    anywhere = pl.BlockSpec(memory_space=pl.ANY)
    return pl.pallas_call(
        kernel,
        out_shape=jax.ShapeDtypeStruct((1, 2, NX, COLS), jnp.bfloat16),
        in_specs=[anywhere] * 5,
        out_specs=pl.BlockSpec(memory_space=pltpu.VMEM),
        scratch_shapes=[
            pltpu.VMEM((CHUNKS, 2, LAYERS, R, NY), jnp.bfloat16),
            pltpu.VMEM((LAYERS, 2, ROWS, NY), jnp.bfloat16),
            pltpu.VMEM((SLABS, NY, 2 * COLS), jnp.bfloat16),
            pltpu.VMEM((2 * NX, NX), jnp.bfloat16),
            pltpu.VMEM((NX, COLS), jnp.float32),
            pltpu.VMEM((2 * R, NY), jnp.bfloat16),
            pltpu.VMEM((CHUNKS, SLABS, R, 2 * COLS), jnp.bfloat16),
            pltpu.VMEM((SLABS, CHUNKS, R, 2 * COLS), jnp.bfloat16),
            pltpu.SemaphoreType.DMA((CHUNKS, 2)),
            pltpu.SemaphoreType.DMA((4,)),
            pltpu.SemaphoreType.DMA((CHUNKS, 2)),
            pltpu.SemaphoreType.DMA((CHUNKS, 2, LAYERS)),
            pltpu.SemaphoreType.DMA((CHUNKS, SLABS)),
            pltpu.SemaphoreType.DMA((CHUNKS, SLABS)),
        ],
        compiler_params=pltpu.CompilerParams(
            collective_id=0, has_side_effects=True, vmem_limit_bytes=48 * 1024 * 1024
        ),
    )(spectra, green, contrast, jnp.asarray(table_y), jnp.asarray(table_x))


def solution(mesh):
    in_specs = (
        P("depth", None, "kslab", None),
        P("depth", None, None, "kslab", None),
        P("depth", None, "kslab"),
    )
    out_specs = P("depth", None, None, "kslab")
    return jax.shard_map(
        on_device, mesh=mesh, in_specs=in_specs, out_specs=out_specs, check_vma=False
    )
```

time: 260 us -> 74.1 us (0.28)
  waiting for transfers between devices: 176 us -> 0 us
  Pallas kernels: 0 us -> 67.9 us
  other arithmetic: 58.1 us -> 0 us
  between operations: 13.5 us -> 0.01 us
  starting transfers between devices: 6.93 us -> 0 us
  local copies, waits for them, and re-layouts: 3.21 us -> 6.02 us
    all_gather x1 -> x0, waiting for transfers between devices: 169 us -> none  [on_device(): lax.all_gather(spectra, 'depth', axis=0, tiled=True).astype(jnp.float32)]
    pallas_call x0 -> x1, Pallas kernels: none -> 67.9 us  [on_device(): pl.pallas_call(kernel, out_shape=jax.ShapeDtypeStruct((1, 2, NX, COLS), j...]
    convert_element_type x4 -> x0, other arithmetic: 33.7 us -> none  [the longest x2 22.3 us: fourier_tables(): (jnp.sin(angles) * factor).astype(jnp.bfloat16)]
    reduce_sum x1 -> x0, other arithmetic: 13 us -> none  [on_device(): jnp.sum(coeffs[:, :, 0] * sources[:, :, 0] - coeffs[:, :, 1] * sources[:,...]
    broadcast_in_dim x1 -> x0, other arithmetic: 11.3 us -> none  [on_device(): lax.all_gather(spectra, 'depth', axis=0, tiled=True).astype(jnp.float32)]
    all_to_all x1 -> x0, starting transfers between devices: 6.93 us -> none  [on_device(): lax.all_to_all(halfway, 'kslab', split_axis=3, concat_axis=2, tiled=True)]
    all_to_all x1 -> x0, waiting for transfers between devices: 6.22 us -> none  [on_device(): lax.all_to_all(halfway, 'kslab', split_axis=3, concat_axis=2, tiled=True)]
    unnamed x6 -> x9, local copies, waits for them, and re-layouts: 1.45 us -> 6.02 us
  transfers between devices with their start and end apart: 2 -> 0, of which waited for: 2 -> 0; matrix products, arithmetic and copies ran while one was open for 13% -> 0% of each run, Pallas kernels for 0% -> 0%
where the time goes in v1:
time: 74.1 us; the launch traced here: 73.9 us
  Pallas kernels  67.9 us (92%)
  local copies, waits for them, and re-layouts  6.02 us (8%)
    pallas_call x1, Pallas kernels, on_device(): pl.pallas_call(kernel, out_shape=jax.ShapeDtypeStruct((1, 2, NX, COLS), j...  67.9 us
    unnamed x9, local copies, waits for them, and re-layouts  6.02 us

profile of v1, /device:TPU:1, one launch (start us, length us, event | category | flops | bytes accessed | tf_op | source)
XLA Modules:
  0.0 73.9 jit_solution(16442511993063752339)
XLA Ops:
  0.0 0.0 copy-start
  0.0 2.2 %copy-done = bf16[8,1024,256]{2,1,0:T(8,128)(2,1)S(1)} copy-done((bf16[8,1024,256]{2,1,0:T(8,128)(2,1)S(1)}, bf16[8,1024,256]{2,1,0:T(8,128)(2,1)}, u32[]{:S(2)}) %copy-start) | copy-done | bytes 4194328
  2.2 0.0 copy-start.1
  2.2 1.2 %copy-done.1 = bf16[1024,512]{1,0:T(8,128)(2,1)S(1)} copy-done((bf16[1024,512]{1,0:T(8,128)(2,1)S(1)}, bf16[1024,512]{1,0:T(8,128)(2,1)}, u32[]{:S(2)}) %copy-start.1) | copy-done | bytes 1048600
  3.4 0.0 copy-start.2
  3.4 0.9 %copy-done.2 = bf16[1,2,64,1024]{3,2,1,0:T(8,128)(2,1)S(1)} copy-done((bf16[1,2,64,1024]{3,2,1,0:T(8,128)(2,1)S(1)}, bf16[1,2,64,1024]{3,2,1,0:T(8,128)(2,1)}, u32[]{:S(2)}) %copy-start.2) | copy-done | bytes 262168
  4.4 0.0 copy-start.3
  4.4 0.9 %copy-done.3 = f32[1,512,128]{2,1,0:T(8,128)S(1)} copy-done((f32[1,512,128]{2,1,0:T(8,128)S(1)}, f32[1,512,128]{2,1,0:T(8,128)}, u32[]{:S(2)}) %copy-start.3) | copy-done | bytes 262168
  5.3 67.9 %shard_map.55 = bf16[1,2,512,128]{3,2,1,0:T(8,128)(2,1)S(1)} custom-call(bf16[1,2,64,1024]{3,2,1,0:T(8,128)(2,1)S(1)} %copy-done.2, bf16[1,32,2,64,1024]{4,3,2,1,0:T(8,128)(2,1)} %green.1, f32[1,512,128]{2,1,0:T(8,128)S(1)} %copy-done.3, bf16[8,1024,256]{2,1,0:T(8,128)(2,1)S(1)} %copy-done, bf16[1024,512]{1,0:T(8,128)(2,1)S(1)} %copy-done.1), custom_call_target="tpu_custom_call" | custom-call | tf_op jit(solution)/shard_map/pallas_call | solution.py:286
  73.2 0.7 copy.7
Async XLA Ops:
  0.0 2.2 %copy-start = (bf16[8,1024,256]{2,1,0:T(8,128)(2,1)S(1)}, bf16[8,1024,256]{2,1,0:T(8,128)(2,1)}, u32[]{:S(2)}) copy-start(bf16[8,1024,256]{2,1,0:T(8,128)(2,1)} %constant.4.clone.table_y) | copy-start | bytes 12582916
  2.2 1.2 %copy-start.1 = (bf16[1024,512]{1,0:T(8,128)(2,1)S(1)}, bf16[1024,512]{1,0:T(8,128)(2,1)}, u32[]{:S(2)}) copy-start(bf16[1024,512]{1,0:T(8,128)(2,1)} %constant.5.clone.table_x) | copy-start | bytes 3145732
  3.4 0.9 %copy-start.2 = (bf16[1,2,64,1024]{3,2,1,0:T(8,128)(2,1)S(1)}, bf16[1,2,64,1024]{3,2,1,0:T(8,128)(2,1)}, u32[]{:S(2)}) copy-start(bf16[1,2,64,1024]{3,2,1,0:T(8,128)(2,1)} %spectra.1) | copy-start | bytes 786436
  4.4 0.9 %copy-start.3 = (f32[1,512,128]{2,1,0:T(8,128)S(1)}, f32[1,512,128]{2,1,0:T(8,128)}, u32[]{:S(2)}) copy-start(f32[1,512,128]{2,1,0:T(8,128)} %contrast.1) | copy-start | bytes 786436

commit v2 on v1

v2 whole, which is shorter than its diff:
```python
import functools
import math

import jax
import jax.numpy as jnp
import ml_dtypes
import numpy as np
from jax import lax
from jax.experimental import pallas as pl
from jax.experimental.pallas import tpu as pltpu
from jax.sharding import PartitionSpec as P

NX = 512
NY = 1024
LAYERS = 32
SLABS = 8
ROWS = NX // SLABS
COLS = NY // SLABS
PIECES = 4
R = ROWS // PIECES
CHUNKS = PIECES // 2
WIDE = 256
CROSSINGS = (6, 6)
MESH = pl.DeviceIdType.MESH


def fourier_tables(length):
    indices = np.arange(length, dtype=np.int64)
    products = indices[:, None] * indices[None, :] % length
    angles = products.astype(np.float64) * (2.0 * math.pi / length)
    factor = 1.0 / math.sqrt(length)
    return (
        (np.cos(angles) * factor).astype(np.float32).astype(ml_dtypes.bfloat16),
        (np.sin(angles) * factor).astype(np.float32).astype(ml_dtypes.bfloat16),
    )


def kernel(
    spectra, green, contrast, table_y, table_x, out,
    held, coeffs, ty, tx, con, partial, summed, outgoing, halves,
    own_sem, load_sem, send_sem, recv_sem, swap_send, swap_recv,
):
    depth = lax.axis_index("depth")
    slab = lax.axis_index("kslab")
    at_x, at_y, at_z = depth // 8, (depth // 2) % 4, depth % 2

    def own_copy(g):
        return pltpu.make_async_copy(
            spectra.at[0, :, pl.ds(g * R, R)], held.at[g, depth], own_sem.at[g]
        )

    for g in range(PIECES):
        own_copy(g).start()

    def layer(h, dz, da, db):
        ca = at_x * (1 - h) + at_y * h
        cb = at_y * (1 - h) + at_x * h
        return (
            (ca + da + 4) % 4 * (8 - 6 * h)
            + (cb + db + 4) % 4 * (2 + 6 * h)
            + (at_z + dz) % 2
        )

    barrier = pltpu.get_barrier_semaphore()
    for other in (
        layer(0, 1, 0, 0), layer(0, 0, 1, 0), layer(0, 0, -1, 0),
        layer(0, 0, 0, 1), layer(0, 0, 0, -1),
    ):
        pl.semaphore_signal(
            barrier, inc=1, device_id={"depth": other}, device_id_type=MESH
        )
    for k in range(1, SLABS):
        pl.semaphore_signal(
            barrier, inc=1, device_id={"kslab": (slab + k) % SLABS}, device_id_type=MESH
        )
    pl.semaphore_wait(barrier, 5 + SLABS - 1)

    def send(g, block, to, half=None):
        ref = held.at[g, block] if half is None else held.at[g, block, half]
        pltpu.make_async_remote_copy(
            src_ref=ref, dst_ref=ref,
            send_sem=send_sem.at[g], recv_sem=recv_sem.at[g, block],
            device_id={"depth": to}, device_id_type=MESH,
        ).start()

    def arrived(g, block):
        ref = held.at[g, block]
        pltpu.make_async_remote_copy(
            src_ref=ref, dst_ref=ref,
            send_sem=send_sem.at[g], recv_sem=recv_sem.at[g, block],
            device_id={"depth": layer(0, 1, 0, 0)}, device_id_type=MESH,
        ).wait_recv()

    def across(g, h, block):
        send(g, block, layer(h, 1, 0, 0))

    def along_a(g, h, block):
        send(g, block, layer(h, 0, 1, 0))
        send(g, block, layer(h, 0, -1, 0))

    def along_b(g, h, block):
        send(g, block, layer(h, 0, 0, 1))
        send(g, block, layer(h, 0, 0, -1))

    def both(c, step):
        def body(h, carry):
            step(2 * c + h, h)
            return carry
        lax.fori_loop(0, 2, body, 0)

    def own(c):
        def step(g, h):
            own_copy(g).wait()
            across(g, h, depth)
            along_a(g, h, depth)
        both(c, step)
        both(c, lambda g, h: along_b(g, h, depth))

    def partner(c):
        def step(g, h):
            block = layer(h, 1, 0, 0)
            arrived(g, block)
            if CROSSINGS[c] == 1:
                along_a(g, h, block)
            if CROSSINGS[c] < 6:
                along_b(g, h, block)
        both(c, step)

    def near(c, dz):
        def step(g, h):
            before, after = layer(h, dz, -1, 0), layer(h, dz, 1, 0)
            in_plane = dz == 0 or CROSSINGS[c] == 1
            arrived(g, before)
            if in_plane:
                send(g, before, layer(h, 0, 1, 0), 0)
            arrived(g, after)
            if in_plane:
                send(g, after, layer(h, 0, -1, 0), 1)
            if dz == 0 and CROSSINGS[c] > 1:
                across(g, h, before)
                across(g, h, after)
            along_b(g, h, before)
            along_b(g, h, after)
        both(c, step)

    def far(c, dz):
        def step(g, h):
            block = layer(h, dz, 2, 0)
            arrived(g, block)
            if dz == 0 and CROSSINGS[c] > 1:
                across(g, h, block)
            along_b(g, h, block)
        both(c, step)

    def relay(c, dz, da):
        def step(g, h):
            before, after = layer(h, dz, da, -1), layer(h, dz, da, 1)
            arrived(g, before)
            send(g, before, layer(h, 0, 0, 1), 0)
            arrived(g, after)
            send(g, after, layer(h, 0, 0, -1), 1)
            if dz == 0 and da == 0 and CROSSINGS[c] == 6:
                across(g, h, before)
                across(g, h, after)
        both(c, step)

    def last(c, dz):
        def step(g, h):
            for da in range(4):
                arrived(g, layer(h, dz, da, 2))
        both(c, step)

    def contract(c, offsets, start=False, end=False):
        def step(g, h):
            rows = pl.ds(pl.multiple_of(g * R, R), R)
            blocks = [layer(h, *offset) for offset in offsets]

            def column(j, carry):
                cs = pl.ds(pl.multiple_of(j * WIDE, WIDE), WIDE)
                re = None if start else partial[h, 0, :, cs]
                im = None if start else partial[h, 1, :, cs]
                for s in blocks:
                    gr = coeffs[s, 0, rows, cs].astype(jnp.float32)
                    gi = coeffs[s, 1, rows, cs].astype(jnp.float32)
                    xr = held[g, s, 0, :, cs].astype(jnp.float32)
                    xi = held[g, s, 1, :, cs].astype(jnp.float32)
                    more_re = gr * xr - gi * xi
                    more_im = gr * xi + gi * xr
                    re = more_re if re is None else re + more_re
                    im = more_im if im is None else im + more_im
                if end:
                    at = pl.multiple_of(h * R, R)
                    summed[pl.ds(at, R), cs] = re.astype(jnp.bfloat16)
                    summed[pl.ds(2 * R + at, R), cs] = im.astype(jnp.bfloat16)
                else:
                    partial[h, 0, :, cs] = re
                    partial[h, 1, :, cs] = im
                return carry
            lax.fori_loop(0, NY // WIDE, column, 0)
        both(c, step)

    def swap(c, to):
        return pltpu.make_async_remote_copy(
            src_ref=outgoing.at[c, to], dst_ref=halves.at[slab, c],
            send_sem=swap_send.at[c, to], recv_sem=swap_recv.at[c, slab],
            device_id={"kslab": to}, device_id_type=MESH,
        )

    def transform_y(c):
        def piece(j):
            both = jnp.dot(summed[...], ty[j], preferred_element_type=jnp.float32)
            re = both[:2 * R, :COLS] - both[2 * R:, COLS:]
            im = both[:2 * R, COLS:] + both[2 * R:, :COLS]
            return jnp.concatenate([re, im], axis=1).astype(jnp.bfloat16)

        def each(k, carry):
            to = (slab + k) % SLABS
            outgoing[c, to] = piece(to)
            swap(c, to).start()
            return carry
        lax.fori_loop(1, SLABS, each, 0)
        halves[slab, c] = piece(slab)

    loads = [
        pltpu.make_async_copy(green.at[0], coeffs, load_sem.at[0]),
        pltpu.make_async_copy(table_y, ty, load_sem.at[1]),
        pltpu.make_async_copy(table_x, tx, load_sem.at[2]),
        pltpu.make_async_copy(contrast.at[0], con, load_sem.at[3]),
    ]

    def start_loads():
        for load in loads:
            load.start()

    def wait_loads():
        for load in loads:
            load.wait()

    early0 = [(0, da, db) for da in (0, 1, -1, 2) for db in (0, 1, -1)]
    early1 = [(1, da, db) for da in (0, 1, -1, 2) for db in (0, 1, -1)]
    late0 = [(0, da, 2) for da in range(4)]
    late1 = [(1, da, 2) for da in range(4)]

    own(0)
    start_loads()
    near(0, 0)
    partner(0)
    far(0, 0)
    relay(0, 0, 0)
    near(0, 1)
    own(1)
    relay(0, 0, 1)
    relay(0, 0, -1)
    far(0, 1)
    near(1, 0)
    relay(0, 0, 2)
    relay(0, 1, 1)
    relay(0, 1, -1)
    wait_loads()
    contract(0, early0, start=True)
    partner(1)
    far(1, 0)
    relay(0, 1, 0)
    relay(0, 1, 2)
    relay(1, 0, 0)
    contract(0, early1)
    near(1, 1)
    last(0, 0)
    contract(0, late0)
    last(0, 1)
    contract(0, late1, end=True)
    relay(1, 0, 1)
    relay(1, 0, -1)
    far(1, 1)
    transform_y(0)
    relay(1, 0, 2)
    relay(1, 1, 1)
    relay(1, 1, -1)
    contract(1, early0, start=True)
    relay(1, 1, 0)
    relay(1, 1, 2)
    contract(1, early1)
    last(1, 0)
    contract(1, late0)
    last(1, 1)
    contract(1, late1, end=True)
    transform_y(1)

    for c in range(CHUNKS):
        def each(k, carry, c=c):
            origin = (slab + k) % SLABS
            pltpu.make_async_remote_copy(
                src_ref=outgoing.at[c, origin], dst_ref=halves.at[origin, c],
                send_sem=swap_send.at[c, origin], recv_sem=swap_recv.at[c, origin],
                device_id={"kslab": origin}, device_id_type=MESH,
            ).wait_recv()
            return carry
        lax.fori_loop(1, SLABS, each, 0)

    incoming = halves[...].reshape(NX, 2 * COLS)
    for i in range(4):
        rows = pl.ds(i * 128, 128)
        low = pl.ds(NX + i * 128, 128)
        by_cos = jnp.dot(tx[rows], incoming, preferred_element_type=jnp.float32)
        by_sin = jnp.dot(tx[low], incoming, preferred_element_type=jnp.float32)
        scale = con[rows]
        out[0, 0, rows] = ((by_cos[:, :COLS] - by_sin[:, COLS:]) * scale).astype(jnp.bfloat16)
        out[0, 1, rows] = ((by_sin[:, :COLS] + by_cos[:, COLS:]) * scale).astype(jnp.bfloat16)

    for g in range(PIECES):
        sent = held.at[g, pl.ds(0, LAYERS - 1)]
        pltpu.make_async_remote_copy(
            src_ref=sent, dst_ref=sent,
            send_sem=send_sem.at[g], recv_sem=recv_sem.at[g, 0],
            device_id={"depth": layer(0, 1, 0, 0)}, device_id_type=MESH,
        ).wait_send()
    for c in range(CHUNKS):
        def each(k, carry, c=c):
            swap(c, (slab + k) % SLABS).wait_send()
            return carry
        lax.fori_loop(1, SLABS, each, 0)


def on_device(spectra, green, contrast):
    cos_y, sin_y = fourier_tables(NY)
    table_y = np.stack(
        [
            np.concatenate(
                [cos_y[:, j * COLS:(j + 1) * COLS], sin_y[:, j * COLS:(j + 1) * COLS]], axis=1
            )
            for j in range(SLABS)
        ]
    )
    cos_x, sin_x = fourier_tables(NX)
    table_x = np.concatenate([cos_x, sin_x], axis=0)
    anywhere = pl.BlockSpec(memory_space=pl.ANY)
    return pl.pallas_call(
        kernel,
        out_shape=jax.ShapeDtypeStruct((1, 2, NX, COLS), jnp.bfloat16),
        in_specs=[anywhere] * 5,
        out_specs=pl.BlockSpec(memory_space=pltpu.VMEM),
        scratch_shapes=[
            pltpu.VMEM((PIECES, LAYERS, 2, R, NY), jnp.bfloat16),
            pltpu.VMEM((LAYERS, 2, ROWS, NY), jnp.bfloat16),
            pltpu.VMEM((SLABS, NY, 2 * COLS), jnp.bfloat16),
            pltpu.VMEM((2 * NX, NX), jnp.bfloat16),
            pltpu.VMEM((NX, COLS), jnp.float32),
            pltpu.VMEM((2, 2, R, NY), jnp.float32),
            pltpu.VMEM((4 * R, NY), jnp.bfloat16),
            pltpu.VMEM((CHUNKS, SLABS, 2 * R, 2 * COLS), jnp.bfloat16),
            pltpu.VMEM((SLABS, CHUNKS, 2 * R, 2 * COLS), jnp.bfloat16),
            pltpu.SemaphoreType.DMA((PIECES,)),
            pltpu.SemaphoreType.DMA((4,)),
            pltpu.SemaphoreType.DMA((PIECES,)),
            pltpu.SemaphoreType.DMA((PIECES, LAYERS)),
            pltpu.SemaphoreType.DMA((CHUNKS, SLABS)),
            pltpu.SemaphoreType.DMA((CHUNKS, SLABS)),
        ],
        compiler_params=pltpu.CompilerParams(
            collective_id=0, has_side_effects=True, vmem_limit_bytes=60 * 1024 * 1024
        ),
    )(spectra, green, contrast, jnp.asarray(table_y), jnp.asarray(table_x))


def solution(mesh):
    in_specs = (
        P("depth", None, "kslab", None),
        P("depth", None, None, "kslab", None),
        P("depth", None, "kslab"),
    )
    out_specs = P("depth", None, None, "kslab")
    return jax.shard_map(
        on_device, mesh=mesh, in_specs=in_specs, out_specs=out_specs, check_vma=False
    )
```

time: 74.1 us -> 62.6 us (0.84)
  Pallas kernels: 67.9 us -> 60.8 us
  local copies, waits for them, and re-layouts: 6.02 us -> 1.67 us
    pallas_call x1, Pallas kernels: 67.9 us -> 60.8 us  [on_device(): pl.pallas_call(kernel, out_shape=jax.ShapeDtypeStruct((1, 2, NX, COLS), j...]
    unnamed x9 -> x1, local copies, waits for them, and re-layouts: 6.02 us -> 1.67 us
where the time goes in v2:
time: 62.6 us; the launch traced here: 62.5 us
  Pallas kernels  60.8 us (97%)
  local copies, waits for them, and re-layouts  1.67 us (3%)
    pallas_call x1, Pallas kernels, on_device(): pl.pallas_call(kernel, out_shape=jax.ShapeDtypeStruct((1, 2, NX, COLS), j...  60.8 us
    unnamed x1, local copies, waits for them, and re-layouts  1.67 us

profile of v2, /device:TPU:1, one launch (start us, length us, event | category | flops | bytes accessed | tf_op | source)
XLA Modules:
  0.0 62.5 jit_solution(1498199062043594430)
XLA Ops:
  0.0 60.8 %shard_map.55 = bf16[1,2,512,128]{3,2,1,0:T(8,128)(2,1)} custom-call(bf16[1,2,64,1024]{3,2,1,0:T(8,128)(2,1)} %spectra.1, bf16[1,32,2,64,1024]{4,3,2,1,0:T(8,128)(2,1)} %green.1, f32[1,512,128]{2,1,0:T(8,128)} %contrast.1, bf16[8,1024,256]{2,1,0:T(8,128)(2,1)} %constant.4.clone.table_y, bf16[1024,512]{1,0:T(8,128)(2,1)} %constant.5.clone.table_x), custom_call_target="tpu_custom_call" | custom-call | tf_op jit(solution)/shard_map/pallas_call | solution.py:337
  60.8 1.7 %copy.7 = bf16[1,2,512,128]{3,2,1,0:T(8,128)(2,1)} copy(bf16[1,2,512,128]{3,2,1,0:T(8,128)(2,1)} %shard_map.55) | data formatting | bytes 524288

commit v3 on v2

--- a/solution.py
+++ b/solution.py
@@ -206,20 +206,35 @@
             device_id={"kslab": to}, device_id_type=MESH,
         )
 
+    def peer(k):
+        pair = k // 2
+        ahead = (2 + pair % 2) * (1 - pair // 2) + (1 - pair % 2) * (pair // 2)
+        chip = (slab // 2 + ahead) % 4
+        return chip * 2 + (slab + 1 + k) % 2
+
     def transform_y(c):
-        def piece(j):
-            both = jnp.dot(summed[...], ty[j], preferred_element_type=jnp.float32)
-            re = both[:2 * R, :COLS] - both[2 * R:, COLS:]
-            im = both[:2 * R, COLS:] + both[2 * R:, :COLS]
-            return jnp.concatenate([re, im], axis=1).astype(jnp.bfloat16)
+        def pair(k):
+            tables = [ty[peer(2 * k)], ty[peer(2 * k + 1)]]
+            result = []
+            for table in tables:
+                both = jnp.dot(summed[...], table, preferred_element_type=jnp.float32)
+                re = both[:2 * R, :COLS] - both[2 * R:, COLS:]
+                im = both[:2 * R, COLS:] + both[2 * R:, :COLS]
+                result.append(jnp.concatenate([re, im], axis=1).astype(jnp.bfloat16))
+            return result
 
         def each(k, carry):
-            to = (slab + k) % SLABS
-            outgoing[c, to] = piece(to)
-            swap(c, to).start()
+            one, two = pair(k)
+            outgoing[c, peer(2 * k)] = one
+            swap(c, peer(2 * k)).start()
+            outgoing[c, peer(2 * k + 1)] = two
+            swap(c, peer(2 * k + 1)).start()
             return carry
-        lax.fori_loop(1, SLABS, each, 0)
-        halves[slab, c] = piece(slab)
+        lax.fori_loop(0, SLABS // 2 - 1, each, 0)
+        one, two = pair(SLABS // 2 - 1)
+        outgoing[c, peer(SLABS - 2)] = one
+        swap(c, peer(SLABS - 2)).start()
+        halves[slab, c] = two
 
     loads = [
         pltpu.make_async_copy(green.at[0], coeffs, load_sem.at[0]),
@@ -243,44 +258,44 @@
 
     own(0)
     start_loads()
+    own(1)
     near(0, 0)
+    near(1, 0)
+    relay(0, 0, 1)
+    near(0, 1)
+    far(0, 0)
     partner(0)
-    far(0, 0)
     relay(0, 0, 0)
-    near(0, 1)
-    own(1)
-    relay(0, 0, 1)
+    partner(1)
     relay(0, 0, -1)
+    relay(0, 1, 1)
+    far(1, 0)
+    relay(0, 0, 2)
     far(0, 1)
-    near(1, 0)
-    relay(0, 0, 2)
-    relay(0, 1, 1)
-    relay(0, 1, -1)
+    near(1, 1)
+    relay(0, 1, 2)
     wait_loads()
     contract(0, early0, start=True)
-    partner(1)
-    far(1, 0)
     relay(0, 1, 0)
-    relay(0, 1, 2)
+    relay(0, 1, -1)
+    last(0, 0)
+    relay(1, 0, -1)
     relay(1, 0, 0)
+    relay(1, 0, 1)
+    relay(1, 0, 2)
     contract(0, early1)
-    near(1, 1)
-    last(0, 0)
+    last(0, 1)
     contract(0, late0)
-    last(0, 1)
+    far(1, 1)
     contract(0, late1, end=True)
-    relay(1, 0, 1)
-    relay(1, 0, -1)
-    far(1, 1)
+    relay(1, 1, 1)
+    contract(1, early0, start=True)
+    relay(1, 1, -1)
     transform_y(0)
-    relay(1, 0, 2)
-    relay(1, 1, 1)
-    relay(1, 1, -1)
-    contract(1, early0, start=True)
+    relay(1, 1, 2)
+    last(1, 0)
     relay(1, 1, 0)
-    relay(1, 1, 2)
     contract(1, early1)
-    last(1, 0)
     contract(1, late0)
     last(1, 1)
     contract(1, late1, end=True)
@@ -357,9 +372,12 @@
             pltpu.SemaphoreType.DMA((CHUNKS, SLABS)),
         ],
         compiler_params=pltpu.CompilerParams(
-            collective_id=0, has_side_effects=True, vmem_limit_bytes=60 * 1024 * 1024
+            collective_id=0, has_side_effects=True, vmem_limit_bytes=44 * 1024 * 1024
         ),
-    )(spectra, green, contrast, jnp.asarray(table_y), jnp.asarray(table_x))
+    )(*[
+        pltpu.with_memory_space_constraint(operand, pltpu.MemorySpace.HBM)
+        for operand in (spectra, green, contrast, jnp.asarray(table_y), jnp.asarray(table_x))
+    ])
 
 
 def solution(mesh):

time: 62.6 us -> 58.3 us (0.931)
  Pallas kernels: 60.8 us -> 57.5 us
  local copies, waits for them, and re-layouts: 1.67 us -> 0.71 us
    pallas_call x1, Pallas kernels: 60.8 us -> 57.5 us  [on_device(): pl.pallas_call(kernel, out_shape=jax.ShapeDtypeStruct((1, 2, NX, COLS), j...]
    unnamed x1, local copies, waits for them, and re-layouts: 1.67 us -> 0.71 us
where the time goes in v3:
time: 58.3 us
  Pallas kernels  57.5 us (99%)
  local copies, waits for them, and re-layouts  0.71 us (1%)
    pallas_call x1, Pallas kernels, on_device(): pl.pallas_call(kernel, out_shape=jax.ShapeDtypeStruct((1, 2, NX, COLS), j...  57.5 us

profile of v3, /device:TPU:1, one launch (start us, length us, event | category | flops | bytes accessed | tf_op | source)
XLA Modules:
  0.0 58.3 jit_solution(8326328036511284026)
XLA Ops:
  0.0 57.5 %shard_map.55 = bf16[1,2,512,128]{3,2,1,0:T(8,128)(2,1)S(1)} custom-call(bf16[1,2,64,1024]{3,2,1,0:T(8,128)(2,1)} %spectra.1, bf16[1,32,2,64,1024]{4,3,2,1,0:T(8,128)(2,1)} %green.1, f32[1,512,128]{2,1,0:T(8,128)} %contrast.1, bf16[8,1024,256]{2,1,0:T(8,128)(2,1)} %constant.4.clone.table_y, bf16[1024,512]{1,0:T(8,128)(2,1)} %constant.5.clone.table_x), custom_call_target="tpu_custom_call" | custom-call | tf_op jit(solution)/shard_map/pallas_call | solution.py:352
  57.5 0.7 %copy.7 = bf16[1,2,512,128]{3,2,1,0:T(8,128)(2,1)} copy(bf16[1,2,512,128]{3,2,1,0:T(8,128)(2,1)S(1)} %shard_map.55) | data formatting | bytes 524288

commit v4 on v0

v4 whole, which is shorter than its diff:
```python
import math

import jax
import jax.numpy as jnp
import ml_dtypes
import numpy as np
from jax import lax
from jax.experimental import pallas as pl
from jax.experimental.pallas import tpu as pltpu
from jax.sharding import PartitionSpec as P

NX = 512
NY = 1024
LAYERS = 32
SLABS = 8
ROWS = NX // SLABS
COLS = NY // SLABS
TILE = 16
SIZES = (32, 32)
STARTS = tuple(sum(SIZES[:c]) for c in range(len(SIZES)))
CHUNKS = len(SIZES)
CROSSINGS = (6, 6)
WIDE = 512
LAST = ((-1, 1), (2, 0))
GROUPS = ((0, 1), (2, 3, 4, 5, 6, 7))
MESH = pl.DeviceIdType.MESH


def fourier_tables(length):
    indices = np.arange(length, dtype=np.int64)
    products = indices[:, None] * indices[None, :] % length
    angles = products.astype(np.float64) * (2.0 * math.pi / length)
    factor = 1.0 / math.sqrt(length)
    return (
        (np.cos(angles) * factor).astype(np.float32).astype(ml_dtypes.bfloat16),
        (np.sin(angles) * factor).astype(np.float32).astype(ml_dtypes.bfloat16),
    )


def width(c):
    return NY * SIZES[c] // (2 * TILE)


def corner(c, h):
    if SIZES[c] == 2 * TILE:
        return STARTS[c] + h * TILE, h * TILE, 0
    return STARTS[c], 0, h * width(c)


def slot(dz, da, db):
    return dz % 2 * 16 + da % 4 * 4 + db % 4


def kernel(spectra, green, contrast, table_y, table_x, out, coeffs, ty, tx, con, partial, summed,
           gathered, own_sem, load_sem, send_sem, recv_sem, swap_send, swap_recv, *buffers):
    held, outgoing, halves = buffers[:CHUNKS], buffers[CHUNKS:2 * CHUNKS], buffers[2 * CHUNKS:]
    depth = lax.axis_index("depth")
    slab = lax.axis_index("kslab")
    at_x, at_y, at_z = depth // 8, (depth // 2) % 4, depth % 2

    def own_copy(c, h):
        row, _, col = corner(c, h)
        return pltpu.make_async_copy(
            spectra.at[0, :, pl.ds(row, TILE), pl.ds(col, width(c))],
            held[c].at[h, 0],
            own_sem.at[c, h],
        )

    def layer(h, dz, da, db):
        dx, dy = (da, db) if h == 0 else (db, da)
        return (at_x + dx + 4) % 4 * 8 + (at_y + dy + 4) % 4 * 2 + (at_z + dz) % 2

    ahead = (layer(0, 0, 1, 0), layer(0, 0, 0, 1))
    behind = (layer(0, 0, -1, 0), layer(0, 0, 0, -1))
    opposite = layer(0, 1, 0, 0)

    barrier = pltpu.get_barrier_semaphore()
    for other in ahead + behind + (opposite,):
        pl.semaphore_signal(
            barrier, inc=1, device_id={"depth": other}, device_id_type=MESH
        )
    for k in range(1, SLABS):
        pl.semaphore_signal(
            barrier, inc=1, device_id={"kslab": (slab + k) % SLABS}, device_id_type=MESH
        )
    for c in range(CHUNKS):
        for h in range(2):
            own_copy(c, h).start()

    pl.semaphore_wait(barrier, 5 + SLABS - 1)

    def send(c, h, offset, axis, step, half=None):
        dz, da, db = offset
        if axis == "z":
            there, to = slot(dz + 1, da, db), opposite
        else:
            at = h if axis == "a" else 1 - h
            to = ahead[at] if step > 0 else behind[at]
            there = slot(dz, da - step, db) if axis == "a" else slot(dz, da, db - step)
        source, target = held[c].at[h, slot(*offset)], held[c].at[h, there]
        if half is not None:
            source, target = held[c].at[h, slot(*offset), half], held[c].at[h, there, half]
        pltpu.make_async_remote_copy(
            src_ref=source, dst_ref=target,
            send_sem=send_sem.at[c, h], recv_sem=recv_sem.at[c, h, there],
            device_id={"depth": to}, device_id_type=MESH,
        ).start()

    def arrived(c, h, *offset):
        ref = held[c].at[h, slot(*offset)]
        pltpu.make_async_remote_copy(
            src_ref=ref, dst_ref=ref,
            send_sem=send_sem.at[c, h], recv_sem=recv_sem.at[c, h, slot(*offset)],
            device_id={"depth": opposite}, device_id_type=MESH,
        ).wait_recv()

    def along(c, h, axis, *offset):
        send(c, h, offset, axis, 1)
        send(c, h, offset, axis, -1)

    def own(c):
        for h in range(2):
            own_copy(c, h).wait()
            send(c, h, (0, 0, 0), "z", 1)
            along(c, h, "a", 0, 0, 0)
        for h in range(2):
            along(c, h, "b", 0, 0, 0)

    def partner(c):
        for h in range(2):
            arrived(c, h, 1, 0, 0)
            if CROSSINGS[c] == 1:
                along(c, h, "a", 1, 0, 0)
            if CROSSINGS[c] < 6:
                along(c, h, "b", 1, 0, 0)

    def near(c, dz):
        in_plane = dz == 0 or CROSSINGS[c] == 1
        for h in range(2):
            arrived(c, h, dz, -1, 0)
            if in_plane:
                send(c, h, (dz, -1, 0), "a", 1, 0)
            arrived(c, h, dz, 1, 0)
            if in_plane:
                send(c, h, (dz, 1, 0), "a", -1, 1)
            if dz == 0 and CROSSINGS[c] > 1:
                send(c, h, (0, -1, 0), "z", 1)
                send(c, h, (0, 1, 0), "z", 1)
            along(c, h, "b", dz, -1, 0)
            along(c, h, "b", dz, 1, 0)

    def far(c, dz):
        for h in range(2):
            arrived(c, h, dz, 2, 0)
            if dz == 0 and CROSSINGS[c] > 1:
                send(c, h, (0, 2, 0), "z", 1)
            along(c, h, "b", dz, 2, 0)

    def relay(c, dz, da):
        for h in range(2):
            arrived(c, h, dz, da, -1)
            send(c, h, (dz, da, -1), "b", 1, 0)
            arrived(c, h, dz, da, 1)
            send(c, h, (dz, da, 1), "b", -1, 1)
            if dz == 0 and da == 0 and CROSSINGS[c] == 6:
                send(c, h, (0, 0, -1), "z", 1)
                send(c, h, (0, 0, 1), "z", 1)

    def last(c, dz):
        for h in range(2):
            for da in range(4):
                arrived(c, h, dz, da, 2)

    def contract(c, offsets, start=False, end=False, parts=(0, 1)):
        for h in parts:
            row, low, col = corner(c, h)
            layers = [layer(h, *offset) for offset in offsets]
            slots = [slot(*offset) for offset in offsets]

            def column(j, carry, h=h, row=row, low=low, col=col, layers=layers, slots=slots):
                cs = pl.ds(pl.multiple_of(j * WIDE, WIDE), WIDE)
                wide = pl.ds(pl.multiple_of(col + j * WIDE, WIDE), WIDE)
                here = pl.ds(low, TILE)
                re = None if start else partial[0, here, wide]
                im = None if start else partial[1, here, wide]
                for s, k in zip(layers, slots):
                    gr = coeffs[s, 0, pl.ds(row, TILE), wide].astype(jnp.float32)
                    gi = coeffs[s, 1, pl.ds(row, TILE), wide].astype(jnp.float32)
                    xr = held[c][h, k, 0, :, cs].astype(jnp.float32)
                    xi = held[c][h, k, 1, :, cs].astype(jnp.float32)
                    more_re = gr * xr - gi * xi
                    more_im = gr * xi + gi * xr
                    re = more_re if re is None else re + more_re
                    im = more_im if im is None else im + more_im
                if end:
                    summed[here, wide] = re.astype(jnp.bfloat16)
                    summed[pl.ds(SIZES[c] + low, TILE), wide] = im.astype(jnp.bfloat16)
                else:
                    partial[0, here, wide] = re
                    partial[1, here, wide] = im
                return carry
            lax.fori_loop(0, width(c) // WIDE, column, 0)

    def finish(c):
        for at, pair in enumerate(LAST):
            for h in range(2):
                for da in pair:
                    arrived(c, h, 1, da, 2)
                offsets = [(1, da, 2) for da in pair]
                contract(c, offsets, end=at == len(LAST) - 1, parts=(h,))

    def peer(k):
        chip = (slab // 2 + (2, 3, 1, 0)[k // 2]) % 4
        return chip * 2 + (slab + 1 + k) % 2

    peers = [peer(k) for k in range(SLABS)]

    def swap(c, k):
        return pltpu.make_async_remote_copy(
            src_ref=outgoing[c].at[k], dst_ref=halves[c].at[slab],
            send_sem=swap_send.at[c, k], recv_sem=swap_recv.at[c, slab],
            device_id={"kslab": peers[k]}, device_id_type=MESH,
        )

    def transform_y(c):
        n = SIZES[c]
        for group in GROUPS:
            results = []
            for k in group:
                both = jnp.dot(summed[:2 * n], ty[peers[k]], preferred_element_type=jnp.float32)
                re = both[:n, :COLS] - both[n:, COLS:]
                im = both[:n, COLS:] + both[n:, :COLS]
                results.append(jnp.concatenate([re, im], axis=1).astype(jnp.bfloat16))
            for k, result in zip(group, results):
                if k < SLABS - 1:
                    outgoing[c][k] = result
                else:
                    halves[c][slab] = result
            for k in group:
                if k < SLABS - 1:
                    swap(c, k).start()

    def swapped(c):
        for k in reversed(range(SLABS - 1)):
            pltpu.make_async_remote_copy(
                src_ref=outgoing[c].at[k], dst_ref=halves[c].at[peers[k]],
                send_sem=swap_send.at[c, k], recv_sem=swap_recv.at[c, peers[k]],
                device_id={"kslab": peers[k]}, device_id_type=MESH,
            ).wait_recv()

    def by_table(c, rows):
        columns = pl.ds(STARTS[c] * SLABS, SIZES[c] * SLABS)
        incoming = halves[c][...].reshape(SLABS * SIZES[c], 2 * COLS)
        return jnp.dot(tx[rows, columns], incoming, preferred_element_type=jnp.float32)

    def gather_x(c):
        for i in range(8):
            rows = pl.ds(i * 128, 128)
            term = by_table(c, rows)
            gathered[rows] = term if c == 0 else gathered[rows] + term

    loads = [
        pltpu.make_async_copy(green.at[0], coeffs, load_sem.at[0]),
        pltpu.make_async_copy(table_y, ty, load_sem.at[1]),
        pltpu.make_async_copy(table_x, tx, load_sem.at[2]),
        pltpu.make_async_copy(contrast.at[0], con, load_sem.at[3]),
    ]

    def start_loads():
        for load in loads:
            load.start()

    def wait_loads():
        for load in loads:
            load.wait()

    early0 = [(0, da, db) for da in (0, 1, -1, 2) for db in (0, 1, -1)]
    early1 = [(1, da, db) for da in (0, 1, -1, 2) for db in (0, 1, -1)]
    late0 = [(0, da, 2) for da in range(4)]
    late1 = [(1, da, 2) for da in range(4)]

    own(1)
    start_loads()
    own(0)
    near(1, 0)
    partner(1)
    near(0, 0)
    near(1, 1)
    far(0, 0)
    partner(0)
    relay(0, 0, 1)
    relay(0, 0, 0)
    relay(0, 0, -1)
    near(0, 1)
    relay(0, 0, 2)
    far(1, 0)
    relay(0, 1, 1)
    far(0, 1)
    wait_loads()
    contract(0, early0, start=True)
    relay(1, 0, 0)
    relay(0, 1, 0)
    relay(0, 1, -1)
    relay(0, 1, 2)
    relay(1, 0, 2)
    far(1, 1)
    contract(0, early1)
    relay(1, 0, -1)
    last(0, 0)
    contract(0, late0)
    relay(1, 0, 1)
    relay(1, 1, -1)
    last(0, 1)
    contract(0, late1, end=True)
    relay(1, 1, 1)
    transform_y(0)
    relay(1, 1, 2)
    relay(1, 1, 0)
    last(1, 0)
    contract(1, early0, start=True)
    contract(1, early1)
    contract(1, late0)
    finish(1)
    transform_y(1)

    for c in range(CHUNKS - 1):
        swapped(c)
        gather_x(c)
    for c in range(CHUNKS):
        for h in range(2):
            sent = held[c].at[h, pl.ds(0, LAYERS - 1)]
            pltpu.make_async_remote_copy(
                src_ref=sent, dst_ref=sent,
                send_sem=send_sem.at[c, h], recv_sem=recv_sem.at[c, h, 0],
                device_id={"depth": opposite}, device_id_type=MESH,
            ).wait_send()
        for k in range(SLABS - 1):
            swap(c, k).wait_send()
    swapped(CHUNKS - 1)
    for i in range(4):
        rows = pl.ds(i * 128, 128)
        low = pl.ds(NX + i * 128, 128)
        by_cos = gathered[rows] + by_table(CHUNKS - 1, rows)
        by_sin = gathered[low] + by_table(CHUNKS - 1, low)
        scale = con[rows]
        out[0, 0, rows] = ((by_cos[:, :COLS] - by_sin[:, COLS:]) * scale).astype(jnp.bfloat16)
        out[0, 1, rows] = ((by_sin[:, :COLS] + by_cos[:, COLS:]) * scale).astype(jnp.bfloat16)


def on_device(spectra, green, contrast):
    cos_y, sin_y = fourier_tables(NY)
    table_y = np.stack(
        [
            np.concatenate(
                [cos_y[:, j * COLS:(j + 1) * COLS], sin_y[:, j * COLS:(j + 1) * COLS]], axis=1
            )
            for j in range(SLABS)
        ]
    )
    cos_x, sin_x = fourier_tables(NX)
    order = np.concatenate(
        [
            (np.arange(SLABS)[:, None] * ROWS + STARTS[c] + np.arange(SIZES[c])[None]).reshape(-1)
            for c in range(CHUNKS)
        ]
    )
    table_x = np.concatenate([cos_x, sin_x], axis=0)[:, order]
    operands = [
        pltpu.with_memory_space_constraint(operand, pltpu.MemorySpace.HBM)
        for operand in (spectra, green, contrast, jnp.asarray(table_y), jnp.asarray(table_x))
    ]
    return pl.pallas_call(
        kernel,
        out_shape=jax.ShapeDtypeStruct((1, 2, NX, COLS), jnp.bfloat16),
        in_specs=[pl.BlockSpec(memory_space=pl.ANY)] * 5,
        out_specs=pl.BlockSpec(memory_space=pltpu.VMEM),
        scratch_shapes=[
            pltpu.VMEM((LAYERS, 2, ROWS, NY), jnp.bfloat16),
            pltpu.VMEM((SLABS, NY, 2 * COLS), jnp.bfloat16),
            pltpu.VMEM((2 * NX, NX), jnp.bfloat16),
            pltpu.VMEM((NX, COLS), jnp.float32),
            pltpu.VMEM((2, 2 * TILE, NY), jnp.float32),
            pltpu.VMEM((4 * TILE, NY), jnp.bfloat16),
            pltpu.VMEM((2 * NX, 2 * COLS), jnp.float32),
            pltpu.SemaphoreType.DMA((CHUNKS, 2)),
            pltpu.SemaphoreType.DMA((4,)),
            pltpu.SemaphoreType.DMA((CHUNKS, 2)),
            pltpu.SemaphoreType.DMA((CHUNKS, 2, LAYERS)),
            pltpu.SemaphoreType.DMA((CHUNKS, SLABS)),
            pltpu.SemaphoreType.DMA((CHUNKS, SLABS)),
        ]
        + [pltpu.VMEM((2, LAYERS, 2, TILE, width(c)), jnp.bfloat16) for c in range(CHUNKS)]
        + [pltpu.VMEM((SLABS, SIZES[c], 2 * COLS), jnp.bfloat16) for c in range(CHUNKS)] * 2,
        compiler_params=pltpu.CompilerParams(
            collective_id=0, has_side_effects=True, vmem_limit_bytes=44 * 1024 * 1024
        ),
    )(*operands)


def solution(mesh):
    in_specs = (
        P("depth", None, "kslab", None),
        P("depth", None, None, "kslab", None),
        P("depth", None, "kslab"),
    )
    out_specs = P("depth", None, None, "kslab")
    return jax.shard_map(
        on_device, mesh=mesh, in_specs=in_specs, out_specs=out_specs, check_vma=False
    )
```

time: 260 us -> 57 us (0.22)
  waiting for transfers between devices: 176 us -> 0 us
  other arithmetic: 58.1 us -> 0 us
  Pallas kernels: 0 us -> 56.2 us
  between operations: 13.5 us -> 0.01 us
  starting transfers between devices: 6.93 us -> 0 us
    all_gather x1 -> x0, waiting for transfers between devices: 169 us -> none  [on_device(): lax.all_gather(spectra, 'depth', axis=0, tiled=True).astype(jnp.float32)]
    pallas_call x0 -> x1, Pallas kernels: none -> 56.2 us  [on_device(): pl.pallas_call(kernel, out_shape=jax.ShapeDtypeStruct((1, 2, NX, COLS), j...]
    convert_element_type x4 -> x0, other arithmetic: 33.7 us -> none  [the longest x2 22.3 us: fourier_tables(): (jnp.sin(angles) * factor).astype(jnp.bfloat16)]
    reduce_sum x1 -> x0, other arithmetic: 13 us -> none  [on_device(): jnp.sum(coeffs[:, :, 0] * sources[:, :, 0] - coeffs[:, :, 1] * sources[:,...]
    broadcast_in_dim x1 -> x0, other arithmetic: 11.3 us -> none  [on_device(): lax.all_gather(spectra, 'depth', axis=0, tiled=True).astype(jnp.float32)]
    all_to_all x1 -> x0, starting transfers between devices: 6.93 us -> none  [on_device(): lax.all_to_all(halfway, 'kslab', split_axis=3, concat_axis=2, tiled=True)]
    all_to_all x1 -> x0, waiting for transfers between devices: 6.22 us -> none  [on_device(): lax.all_to_all(halfway, 'kslab', split_axis=3, concat_axis=2, tiled=True)]
  transfers between devices with their start and end apart: 2 -> 0, of which waited for: 2 -> 0; matrix products, arithmetic and copies ran while one was open for 13% -> 0% of each run, Pallas kernels for 0% -> 0%
where the time goes in v4:
time: 57 us; the launch traced here: 56.9 us
  Pallas kernels  56.2 us (99%)
  local copies, waits for them, and re-layouts  0.71 us (1%)
    pallas_call x1, Pallas kernels, on_device(): pl.pallas_call(kernel, out_shape=jax.ShapeDtypeStruct((1, 2, NX, COLS), j...  56.2 us

profile of v4, /device:TPU:1, one launch (start us, length us, event | category | flops | bytes accessed | tf_op | source)
XLA Modules:
  0.0 56.9 jit_solution(4146477152483942465)
XLA Ops:
  0.0 56.2 %shard_map.55 = bf16[1,2,512,128]{3,2,1,0:T(8,128)(2,1)S(1)} custom-call(bf16[1,2,64,1024]{3,2,1,0:T(8,128)(2,1)} %spectra.1, bf16[1,32,2,64,1024]{4,3,2,1,0:T(8,128)(2,1)} %green.1, f32[1,512,128]{2,1,0:T(8,128)} %contrast.1, bf16[8,1024,256]{2,1,0:T(8,128)(2,1)} %constant.4.clone.table_y, bf16[1024,512]{1,0:T(8,128)(2,1)} %constant.5.clone.table_x), custom_call_target="tpu_custom_call" | custom-call | tf_op jit(solution)/shard_map/pallas_call | solution.py:372
  56.2 0.7 %copy.7 = bf16[1,2,512,128]{3,2,1,0:T(8,128)(2,1)} copy(bf16[1,2,512,128]{3,2,1,0:T(8,128)(2,1)S(1)} %shard_map.55) | data formatting | bytes 524288

commit v5 on v4

--- a/solution.py
+++ b/solution.py
@@ -22,7 +22,7 @@
 CROSSINGS = (6, 6)
 WIDE = 512
 LAST = ((-1, 1), (2, 0))
-GROUPS = ((0, 1), (2, 3, 4, 5, 6, 7))
+GROUPS = ((0, 1), (2, 3, 4, 5), (6, 7))
 MESH = pl.DeviceIdType.MESH
 
 

time: 57 us -> 57.3 us (level)
  no operation moved by 1% of the time
where the time goes in v5:
time: 57.3 us; the launch traced here: 57.2 us
  Pallas kernels  56.5 us (99%)
  local copies, waits for them, and re-layouts  0.71 us (1%)
    pallas_call x1, Pallas kernels, on_device(): pl.pallas_call(kernel, out_shape=jax.ShapeDtypeStruct((1, 2, NX, COLS), j...  56.5 us

profile of v5, /device:TPU:1, one launch (start us, length us, event | category | flops | bytes accessed | tf_op | source)
XLA Modules:
  0.0 57.2 jit_solution(5299556356275440443)
XLA Ops:
  0.0 56.5 %shard_map.55 = bf16[1,2,512,128]{3,2,1,0:T(8,128)(2,1)S(1)} custom-call(bf16[1,2,64,1024]{3,2,1,0:T(8,128)(2,1)} %spectra.1, bf16[1,32,2,64,1024]{4,3,2,1,0:T(8,128)(2,1)} %green.1, f32[1,512,128]{2,1,0:T(8,128)} %contrast.1, bf16[8,1024,256]{2,1,0:T(8,128)(2,1)} %constant.4.clone.table_y, bf16[1024,512]{1,0:T(8,128)(2,1)} %constant.5.clone.table_x), custom_call_target="tpu_custom_call" | custom-call | tf_op jit(solution)/shard_map/pallas_call | solution.py:372
  56.5 0.7 %copy.7 = bf16[1,2,512,128]{3,2,1,0:T(8,128)(2,1)} copy(bf16[1,2,512,128]{3,2,1,0:T(8,128)(2,1)S(1)} %shard_map.55) | data formatting | bytes 524288
